TPU v7x, 256 devices: a whole 4x4x8 slice. The times are simulated.
256 devices in a mesh: batch: 2 (over z_lo), seq: 128 (over z_hi, y, x, core).
Axes of the slice: x: 4, y: 4, z: 8 (z_hi: 4, z_lo: 2; z = z_hi * 2 + z_lo), core: 2. Of those that a mesh axis runs over, the one named last changes fastest.
Arguments:
- signal: bfloat16 [2, 262144, 384], P('batch', 'seq'), may hold values from -6 to 6
- conv_weight: float32 [4, 384], replicated, may hold values from -2.5 to 2.5
- first_factor: bfloat16 [512, 512, 512], P('seq'), may hold values from -0.25 to 0.25
- second_factor: bfloat16 [512, 512, 512], P('seq'), may hold values from -0.25 to 0.25
- grad_output: bfloat16 [2, 262144, 384], P('batch', 'seq'), may hold values from -3 to 3
Outputs:
- grad_signal: bfloat16 [2, 262144, 384], P('batch', 'seq')
- grad_first: bfloat16 [512, 512, 512], P('seq', 'batch')
- grad_second: bfloat16 [512, 512, 512], P('seq', 'batch')
All inputs are finite; a program needn't handle non-finite values.
Results may differ from a plain program's by a relative error of at most 0.0065.
Values may be sent and summed in bfloat16 or wider, within the bound.
A program may use at most 128 MiB of HBM per device.

v0:
```python
import jax
import jax.numpy as jnp
from jax import lax
from jax.sharding import PartitionSpec as P


def passed_along(value, axis, steps):
    count = lax.axis_size(axis)
    initial, last = (max(0, -steps), min(count, count - steps))
    return lax.ppermute(value, axis, [(source, source + steps) for source in range(initial, last)])


def body(signal, conv_weight, first_factor, second_factor, grad_output):
    seq_count, tok_rows, channels = signal.shape
    blocks = first_factor.shape[0]
    block_order = first_factor.shape[1]
    col_blocks = second_factor.shape[0]
    block_count = second_factor.shape[1]
    tap_count = conv_weight.shape[0]
    previous = passed_along(signal[:, tok_rows - (tap_count - 1) :, :], "seq", 1)
    padded_in = jnp.concatenate([previous, signal], axis=1).astype(jnp.float32)
    conv_out = sum(
        (
            conv_weight[r][None, None, :]
            * padded_in[:, tap_count - 1 - r : tap_count - 1 - r + tok_rows, :]
            for r in range(tap_count)
        )
    )
    gate_val = jax.nn.sigmoid(conv_out)
    hidden = (conv_out * gate_val).astype(jnp.bfloat16)
    hidden_blocks = hidden.reshape(seq_count, blocks, block_order, channels)
    mixed = jnp.einsum(
        "ikj,sijd->sikd", first_factor, hidden_blocks, preferred_element_type=jnp.float32
    ).astype(jnp.bfloat16)
    columns = lax.all_to_all(mixed, "seq", split_axis=2, concat_axis=1, tiled=True)
    upstream = grad_output.reshape(seq_count, col_blocks, block_count, channels)
    grad_mixed = jnp.einsum(
        "kmi,skmd->sikd", second_factor, upstream, preferred_element_type=jnp.float32
    ).astype(jnp.bfloat16)
    grad_second = jnp.einsum(
        "skmd,sikd->kmi", upstream, columns, preferred_element_type=jnp.float32
    )
    grad_rows = lax.all_to_all(grad_mixed, "seq", split_axis=1, concat_axis=2, tiled=True)
    grad_hidden = jnp.einsum(
        "ikj,sikd->sijd", first_factor, grad_rows, preferred_element_type=jnp.float32
    ).reshape(seq_count, tok_rows, channels)
    grad_conv = (grad_hidden * gate_val * (1.0 + conv_out * (1.0 - gate_val))).astype(jnp.bfloat16)
    following = passed_along(grad_conv[:, : tap_count - 1, :], "seq", -1)
    extended = jnp.concatenate([grad_conv, following], axis=1).astype(jnp.float32)
    grad_signal = sum(
        (conv_weight[r][None, None, :] * extended[:, r : r + tok_rows, :] for r in range(tap_count))
    ).astype(jnp.bfloat16)
    grad_first = jnp.einsum(
        "sikd,sijd->ikj", grad_rows, hidden_blocks, preferred_element_type=jnp.float32
    )
    total_first, total_second = (
        lax.psum(grad_first.astype(jnp.bfloat16), "batch").astype(jnp.float32),
        lax.psum(grad_second.astype(jnp.bfloat16), "batch").astype(jnp.float32),
    )
    batch_index = lax.axis_index("batch")
    half_first = total_first.shape[1] // lax.axis_size("batch")
    half_second = total_second.shape[1] // lax.axis_size("batch")
    share_first = lax.dynamic_slice_in_dim(total_first, batch_index * half_first, half_first, 1)
    share_second = lax.dynamic_slice_in_dim(total_second, batch_index * half_second, half_second, 1)
    return (grad_signal, share_first.astype(jnp.bfloat16), share_second.astype(jnp.bfloat16))


def solution(mesh):
    placed = (
        P("batch", "seq", None),
        P(),
        P("seq", None, None),
        P("seq", None, None),
        P("batch", "seq", None),
    )
    return jax.shard_map(
        body,
        mesh=mesh,
        in_specs=placed,
        out_specs=(P("batch", "seq", None), P("seq", "batch", None), P("seq", "batch", None)),
        check_vma=False,
    )
```

profile of v0, /device:TPU:1, one launch (start us, length us, event | category | flops | bytes accessed | tf_op | source)
XLA Modules:
  0.0 269.5 jit_solution(10913673899404368837)
XLA Ops:
  7.2 4.4 %fusion.9 = bf16[1,512,4,384]{1,3,2,0:T(8,128)(2,1)} fusion(bf16[4,512,384]{2,1,0:T(8,128)(2,1)} %bitcast.39, bf16[4,512,512]{2,1,0:T(8,128)(2,1)} %param.8), kind=kOutput, calls=%fused_computation.29 | convolution fusion | flops 806092800 | bytes 5242880 | tf_op jit(solution)/shard_map/kmi,skmd->sikd/dot_general | solution.py:37
  11.6 3.8 %copy.25 = bf16[1,512,4,384]{3,2,0,1:T(4,128)(2,1)} copy(bf16[1,512,4,384]{1,3,2,0:T(8,128)(2,1)} %fusion.9) | data formatting | bytes 3145728 | tf_op jit(solution)/shard_map/convert_element_type | solution.py:39
  15.3 16.9 %all-to-all-start = ((bf16[1,512,4,384]{3,2,0,1:T(4,128)(2,1)}), bf16[1,512,4,384]{3,2,0,1:T(4,128)(2,1)}, u32[]{:S(2)}, u32[]{:S(2)}) async-start(bf16[1,512,4,384]{3,2,0,1:T(4,128)(2,1)} %copy.25), calls=%async_computation | async-start | bytes 3145728 | tf_op jit(solution)/shard_map/all_to_all | solution.py:43
  33.0 3.5 %collective-permute-start = (bf16[1,3,384]{2,1,0:T(4,128)(2,1)S(1)}, bf16[1,3,384]{2,1,0:T(4,128)(2,1)S(1)}, u32[]{:S(2)}, u32[]{:S(2)}) collective-permute-start(bf16[1,3,384]{2,1,0:T(4,128)(2,1)S(1)} %slice.47), channel_id=1, source_target_pairs={{0,1},{1,2},{2,3},{3,4},{4,5},{5,6},{6,7},{7,8},{8,9},{9,10},{10,1... | collective-permute-start | bytes 6920 | tf_op jit(solution)/shard_map/ppermute | solution.py:10
  37.2 1.7 maximum_convert_fusion
  39.0 3.1 %multiply_convert_fusion = (bf16[1,2048,384]{2,1,0:T(8,128)(2,1)S(1)}, f32[1,2048,384]{2,1,0:T(8,128)}) fusion(f32[1,2051,384]{2,1,0:T(8,128)S(1)} %maximum_convert_fusion, f32[384]{0:T(512)S(1)} %get-tuple-element.14, f32[384]{0:T(512)S(1)} %get-tuple-element.15, f32[384]{0:T(512)S(1)} %get-tuple-element.13, f32[384]{0:T(512)S(1)} %get-tuple-element.12), kind=kLoop, calls=%fused_computation.18 | loop fusion | flops 9437184 | bytes 17307648 | tf_op jit(solution)/shard_map/convert_element_type | solution.py:30
  43.3 2.3 fusion.10
  45.6 3.8 %copy.31 = bf16[1,4,512,384]{3,1,0,2:T(4,128)(2,1)} copy(bf16[1,4,512,384]{2,3,1,0:T(8,128)(2,1)} %fusion.10) | data formatting | bytes 3145728 | tf_op jit(solution)/shard_map/convert_element_type | solution.py:34
  49.4 23.6 %all-to-all-done = bf16[1,512,4,384]{3,2,0,1:T(4,128)(2,1)} async-done(((bf16[1,512,4,384]{3,2,0,1:T(4,128)(2,1)}), bf16[1,512,4,384]{3,2,0,1:T(4,128)(2,1)}, u32[]{:S(2)}, u32[]{:S(2)}) %all-to-all-start) | async-done | bytes 1572896 | tf_op jit(solution)/shard_map/all_to_all | solution.py:43
  73.0 17.0 %all-to-all-start.1 = ((bf16[1,4,512,384]{3,1,0,2:T(4,128)(2,1)}), bf16[1,4,512,384]{3,1,0,2:T(4,128)(2,1)}, u32[]{:S(2)}, u32[]{:S(2)}) async-start(bf16[1,4,512,384]{3,1,0,2:T(4,128)(2,1)} %copy.31), calls=%async_computation.1 | async-start | bytes 3145728 | tf_op jit(solution)/shard_map/all_to_all | solution.py:35
  90.2 2.1 copy.26
  93.5 2.6 convolution_convert_fusion
  96.1 30.5 %all-to-all-done.1 = bf16[1,4,512,384]{3,1,0,2:T(4,128)(2,1)} async-done(((bf16[1,4,512,384]{3,1,0,2:T(4,128)(2,1)}), bf16[1,4,512,384]{3,1,0,2:T(4,128)(2,1)}, u32[]{:S(2)}, u32[]{:S(2)}) %all-to-all-start.1) | async-done | bytes 1572896 | tf_op jit(solution)/shard_map/all_to_all | solution.py:35
  126.6 3.1 %copy.32 = bf16[1,128,4,4,384]{4,2,1,3,0:T(4,128)(2,1)} copy(bf16[1,128,4,4,384]{4,2,3,1,0:T(4,128)(2,1)} %bitcast.13) | data formatting | bytes 3145728 | tf_op jit(solution)/shard_map/all_to_all | solution.py:35
  129.7 3.7 %reshape.110 = bf16[512,4,384]{2,0,1:T(8,128)(2,1)} reshape(bf16[1,128,4,4,384]{4,2,1,3,0:T(4,128)(2,1)} %copy.32) | data formatting | bytes 3145728 | tf_op jit(solution)/shard_map/reshape.23
  133.4 4.6 %convert_bitcast_fusion = bf16[4,512,512]{1,2,0:T(8,128)(2,1)} fusion(bf16[512,4,384]{2,0,1:T(8,128)(2,1)} %reshape.110, bf16[4,512,384]{2,1,0:T(8,128)(2,1)} %bitcast.40), kind=kOutput, calls=%fused_computation.21 | convolution fusion | flops 806354944 | bytes 5242880 | tf_op jit(solution)/shard_map/skmd,sikd->kmi/dot_general | solution.py:40
  138.0 4.1 %convolution_bitcast_fusion = f32[1,4,512,384]{2,3,1,0:T(8,128)} fusion(bf16[4,512,512]{2,1,0:T(8,128)(2,1)S(1)} %copy-done, bf16[4,512,384]{2,0,1:T(4,128)(2,1)} %bitcast.42), kind=kOutput, calls=%fused_computation.24 | convolution fusion | flops 805306368 | bytes 6815744 | tf_op jit(solution)/shard_map/ikj,sikd->sijd/dot_general | solution.py:44
  142.2 3.6 %copy.28 = f32[1,4,512,384]{3,2,1,0:T(8,128)} copy(f32[1,4,512,384]{2,3,1,0:T(8,128)} %convolution_bitcast_fusion) | data formatting | bytes 6291456 | tf_op jit(solution)/shard_map/ikj,sikd->sijd/transpose | solution.py:44
  145.7 4.0 %fusion.8 = bf16[1,2048,384]{2,1,0:T(8,128)(2,1)S(1)} fusion(f32[1,4,512,384]{3,2,1,0:T(8,128)} %copy.28, f32[1,2048,384]{2,1,0:T(8,128)} %get-tuple-element.19), kind=kLoop, calls=%fused_computation.17 | loop fusion | flops 7077888 | bytes 7864320 | tf_op jit(solution)/shard_map/convert_element_type | solution.py:47
  150.8 10.2 %collective-permute-start.1 = (bf16[1,3,384]{2,1,0:T(4,128)(2,1)S(1)}, bf16[1,3,384]{2,1,0:T(4,128)(2,1)S(1)}, u32[]{:S(2)}, u32[]{:S(2)}) collective-permute-start(bf16[1,3,384]{2,1,0:T(4,128)(2,1)S(1)} %slice.64), channel_id=1, source_target_pairs={{1,0},{2,1},{3,2},{4,3},{5,4},{6,5},{7,6},{8,7},{9,8},{10,9},{11,1... | collective-permute-start | bytes 6920 | tf_op jit(solution)/shard_map/ppermute | solution.py:10
  161.9 1.6 maximum_convert_fusion.1
  163.5 2.5 fusion.1
  166.1 91.7 %all-reduce.3.cloned.1.call-done = (bf16[4,512,512]{2,1,0:T(8,128)(2,1)}, bf16[4,512,512]{1,2,0:T(8,128)(2,1)}) async-done(((bf16[4,512,512]{2,1,0:T(8,128)(2,1)}, bf16[4,512,512]{1,2,0:T(8,128)(2,1)}), (bf16[4,512,512]{2,1,0:T(8,128)(2,1)}, bf16[4,512,512]{1,2,0:T(8,128)(2,1)})) %all-reduce.3.cloned.1.call-update) | async-done | bytes 4194320 | tf_op jit(solution)/shard_map/psum | solution.py:57
  260.4 2.3 convert_convert_fusion.1
  (21 shorter events, 8.6 us)
Async XLA Ops:
  7.2 36.1 %copy-start = (bf16[4,512,512]{2,1,0:T(8,128)(2,1)S(1)}, bf16[4,512,512]{2,1,0:T(8,128)(2,1)}, u32[]{:S(2)}) copy-start(bf16[4,512,512]{2,1,0:T(8,128)(2,1)} %param.7) | copy-start | bytes 6291460
  15.3 21.2 %copy-start.5 = (f32[4,384]{1,0:T(4,128)S(1)}, f32[4,384]{1,0:T(4,128)}, u32[]{:S(2)}) copy-start(f32[4,384]{1,0:T(4,128)} %param.6) | copy-start | bytes 18436
  15.3 57.7 %all-to-all-start = ((bf16[1,512,4,384]{3,2,0,1:T(4,128)(2,1)}), bf16[1,512,4,384]{3,2,0,1:T(4,128)(2,1)}, u32[]{:S(2)}, u32[]{:S(2)}) async-start(bf16[1,512,4,384]{3,2,0,1:T(4,128)(2,1)} %copy.25), calls=%async_computation | async-start | bytes 3145728 | tf_op jit(solution)/shard_map/all_to_all | solution.py:43
  33.0 4.3 %collective-permute-start = (bf16[1,3,384]{2,1,0:T(4,128)(2,1)S(1)}, bf16[1,3,384]{2,1,0:T(4,128)(2,1)S(1)}, u32[]{:S(2)}, u32[]{:S(2)}) collective-permute-start(bf16[1,3,384]{2,1,0:T(4,128)(2,1)S(1)} %slice.47), channel_id=1, source_target_pairs={{0,1},{1,2},{2,3},{3,4},{4,5},{5,6},{6,7},{7,8},{8,9},{9,10},{10,1... | collective-permute-start | bytes 6920 | tf_op jit(solution)/shard_map/ppermute | solution.py:10
  42.1 1.2 copy-start.3
  73.0 53.6 %all-to-all-start.1 = ((bf16[1,4,512,384]{3,1,0,2:T(4,128)(2,1)}), bf16[1,4,512,384]{3,1,0,2:T(4,128)(2,1)}, u32[]{:S(2)}, u32[]{:S(2)}) async-start(bf16[1,4,512,384]{3,1,0,2:T(4,128)(2,1)} %copy.31), calls=%async_computation.1 | async-start | bytes 3145728 | tf_op jit(solution)/shard_map/all_to_all | solution.py:35
  90.0 167.8 %all-reduce.3.cloned.1.call-start = ((), (), s32[]{:S(2)}) async-start(), calls=%async_computation.2 | async-start | bytes 8388608 | tf_op jit(solution)/shard_map/psum | solution.py:57
  90.2 3.3 %copy-start.4 = (bf16[1,2048,384]{2,1,0:T(8,128)(2,1)S(1)}, bf16[1,2048,384]{2,1,0:T(8,128)(2,1)}, u32[]{:S(2)}) copy-start(bf16[1,2048,384]{2,1,0:T(8,128)(2,1)} %copy-done.3) | copy-start | bytes 4718596
  92.4 1.1 copy-start.2
  149.7 1.1 copy-start.1
  150.8 11.1 %collective-permute-start.1 = (bf16[1,3,384]{2,1,0:T(4,128)(2,1)S(1)}, bf16[1,3,384]{2,1,0:T(4,128)(2,1)S(1)}, u32[]{:S(2)}, u32[]{:S(2)}) collective-permute-start(bf16[1,3,384]{2,1,0:T(4,128)(2,1)S(1)} %slice.64), channel_id=1, source_target_pairs={{1,0},{2,1},{3,2},{4,3},{5,4},{6,5},{7,6},{8,7},{9,8},{10,9},{11,1... | collective-permute-start | bytes 6920 | tf_op jit(solution)/shard_map/ppermute | solution.py:10
Sparse Core Ops, SparseCore 0:
  138.2 119.5 all-reduce.2
where the time goes:
time: 270 us
  waiting for transfers between devices  147 us (54%)
  starting transfers between devices  47.9 us (18%)
  local copies, waits for them, and re-layouts  25.7 us (10%)
  matrix products  18 us (7%)
  other arithmetic  16.5 us (6%)
  between operations  14.1 us (5%)
    psum x1, waiting for transfers between devices, body(): lax.psum(grad_first.astype(jnp.bfloat16), 'batch').astype(jnp.float32)  91.7 us
    all_to_all x1, waiting for transfers between devices, body(): lax.all_to_all(mixed, 'seq', split_axis=2, concat_axis=1, tiled=True)  30.5 us
    all_to_all x1, waiting for transfers between devices, body(): lax.all_to_all(grad_mixed, 'seq', split_axis=1, concat_axis=2, tiled=True)  23.6 us
    all_to_all x1, starting transfers between devices, body(): lax.all_to_all(mixed, 'seq', split_axis=2, concat_axis=1, tiled=True)  17 us
    all_to_all x1, starting transfers between devices, body(): lax.all_to_all(grad_mixed, 'seq', split_axis=1, concat_axis=2, tiled=True)  16.9 us
    ppermute x2, starting transfers between devices, passed_along(): lax.ppermute(value, axis, [(source, source + steps) for source in range(i...  13.8 us
  transfers between devices with their start and end apart: 5, of which 5 were waited for; matrix products, arithmetic and copies ran while one was open for 12% of the time, Pallas kernels for 0%

commit v1 on v0

--- a/solution.py
+++ b/solution.py
@@ -2,6 +2,11 @@
 import jax.numpy as jnp
 from jax import lax
 from jax.sharding import PartitionSpec as P
+
+
+def guide_the_plane(arr_in):
+    carry = lax.all_gather(arr_in, "batch").sum(axis=0)
+    return carry
 
 
 def passed_along(value, axis, steps):
@@ -54,7 +59,7 @@
         "sikd,sijd->ikj", grad_rows, hidden_blocks, preferred_element_type=jnp.float32
     )
     total_first, total_second = (
-        lax.psum(grad_first.astype(jnp.bfloat16), "batch").astype(jnp.float32),
+        guide_the_plane(grad_first.astype(jnp.bfloat16)).astype(jnp.float32),
         lax.psum(grad_second.astype(jnp.bfloat16), "batch").astype(jnp.float32),
     )
     batch_index = lax.axis_index("batch")

time: 270 us -> 269 us (level)
  starting transfers between devices: 47.9 us -> 36.2 us
  other arithmetic: 16.5 us -> 21.5 us
  waiting for transfers between devices: 147 us -> 152 us
    psum x1, waiting for transfers between devices: 91.7 us -> 25.2 us  [body(): lax.psum(grad_second.astype(jnp.bfloat16), 'batch').astype(jnp.float32)]
    all_gather x0 -> x1, waiting for transfers between devices: none -> 61.6 us  [guide_the_plane(): carry = lax.all_gather(arr_in, 'batch').sum(axis=0)]
    all_to_all x1, waiting for transfers between devices: 23.6 us -> 31.8 us  [body(): lax.all_to_all(grad_mixed, 'seq', split_axis=1, concat_axis=2, tiled=True)]
    all_to_all x1, starting transfers between devices: 16.9 us -> 9.76 us  [body(): lax.all_to_all(grad_mixed, 'seq', split_axis=1, concat_axis=2, tiled=True)]
    ppermute x2, starting transfers between devices: 13.8 us -> 8.58 us  [passed_along(): lax.ppermute(value, axis, [(source, source + steps) for source in range(i...]
    reduce_sum x0 -> x1, other arithmetic: none -> 4.93 us  [guide_the_plane(): carry = lax.all_gather(arr_in, 'batch').sum(axis=0)]
  transfers between devices with their start and end apart: 5 -> 6, of which waited for: 5 -> 5; matrix products, arithmetic and copies ran while one was open for 12% -> 16% of each run, Pallas kernels for 0% -> 0%
where the time goes in v1:
time: 269 us; the launch traced here: 268 us
  waiting for transfers between devices  152 us (57%)
  starting transfers between devices  36.2 us (13%)
  local copies, waits for them, and re-layouts  26.7 us (10%)
  other arithmetic  21.5 us (8%)
  matrix products  17.8 us (7%)
  between operations  14.1 us (5%)
    all_gather x1, waiting for transfers between devices, guide_the_plane(): carry = lax.all_gather(arr_in, 'batch').sum(axis=0)  61.6 us
    all_to_all x1, waiting for transfers between devices, body(): lax.all_to_all(mixed, 'seq', split_axis=2, concat_axis=1, tiled=True)  32.6 us
    all_to_all x1, waiting for transfers between devices, body(): lax.all_to_all(grad_mixed, 'seq', split_axis=1, concat_axis=2, tiled=True)  31.8 us
    psum x1, waiting for transfers between devices, body(): lax.psum(grad_second.astype(jnp.bfloat16), 'batch').astype(jnp.float32)  25.2 us
    all_to_all x1, starting transfers between devices, body(): lax.all_to_all(mixed, 'seq', split_axis=2, concat_axis=1, tiled=True)  17.6 us
    all_to_all x1, starting transfers between devices, body(): lax.all_to_all(grad_mixed, 'seq', split_axis=1, concat_axis=2, tiled=True)  9.76 us
    ppermute x2, starting transfers between devices, passed_along(): lax.ppermute(value, axis, [(source, source + steps) for source in range(i...  8.58 us
  transfers between devices with their start and end apart: 6, of which 5 were waited for; matrix products, arithmetic and copies ran while one was open for 16% of the time, Pallas kernels for 0%

profile of v1, /device:TPU:1, one launch (start us, length us, event | category | flops | bytes accessed | tf_op | source)
XLA Modules:
  0.0 268.4 jit_solution(9329229375404878717)
XLA Ops:
  8.0 4.5 %collective-permute-start = (bf16[1,3,384]{2,1,0:T(4,128)(2,1)S(1)}, bf16[1,3,384]{2,1,0:T(4,128)(2,1)S(1)}, u32[]{:S(2)}, u32[]{:S(2)}) collective-permute-start(bf16[1,3,384]{2,1,0:T(4,128)(2,1)S(1)} %slice.47), channel_id=1, source_target_pairs={{0,1},{1,2},{2,3},{3,4},{4,5},{5,6},{6,7},{7,8},{8,9},{9,10},{10,1... | collective-permute-start | bytes 6920 | tf_op jit(solution)/shard_map/ppermute | solution.py:15
  15.1 3.1 %multiply_convert_fusion = (bf16[1,2048,384]{2,1,0:T(8,128)(2,1)S(1)}, f32[1,2048,384]{2,1,0:T(8,128)}) fusion(f32[1,2051,384]{2,1,0:T(8,128)S(1)} %maximum_convert_fusion, f32[384]{0:T(512)S(1)} %get-tuple-element.14, f32[384]{0:T(512)S(1)} %get-tuple-element.15, f32[384]{0:T(512)S(1)} %get-tuple-element.13, f32[384]{0:T(512)S(1)} %get-tuple-element.12), kind=kLoop, calls=%fused_computation.18 | loop fusion | flops 9437184 | bytes 17307648 | tf_op jit(solution)/shard_map/convert_element_type | solution.py:35
  19.4 2.3 fusion.10
  21.7 3.8 %copy.31 = bf16[1,4,512,384]{3,1,0,2:T(4,128)(2,1)} copy(bf16[1,4,512,384]{2,3,1,0:T(8,128)(2,1)} %fusion.10) | data formatting | bytes 3145728 | tf_op jit(solution)/shard_map/convert_element_type | solution.py:39
  25.5 17.6 %all-to-all-start.1 = ((bf16[1,4,512,384]{3,1,0,2:T(4,128)(2,1)}), bf16[1,4,512,384]{3,1,0,2:T(4,128)(2,1)}, u32[]{:S(2)}, u32[]{:S(2)}) async-start(bf16[1,4,512,384]{3,1,0,2:T(4,128)(2,1)} %copy.31), calls=%async_computation.1 | async-start | bytes 3145728 | tf_op jit(solution)/shard_map/all_to_all | solution.py:40
  43.1 4.2 %fusion.9 = bf16[1,512,4,384]{1,3,2,0:T(8,128)(2,1)} fusion(bf16[4,512,384]{2,1,0:T(8,128)(2,1)} %bitcast.40, bf16[4,512,512]{2,1,0:T(8,128)(2,1)} %param.8), kind=kOutput, calls=%fused_computation.29 | convolution fusion | flops 806092800 | bytes 5242880 | tf_op jit(solution)/shard_map/kmi,skmd->sikd/dot_general | solution.py:42
  47.3 3.8 %copy.25 = bf16[1,512,4,384]{3,2,0,1:T(4,128)(2,1)} copy(bf16[1,512,4,384]{1,3,2,0:T(8,128)(2,1)} %fusion.9) | data formatting | bytes 3145728 | tf_op jit(solution)/shard_map/convert_element_type | solution.py:44
  51.2 32.6 %all-to-all-done.1 = bf16[1,4,512,384]{3,1,0,2:T(4,128)(2,1)} async-done(((bf16[1,4,512,384]{3,1,0,2:T(4,128)(2,1)}), bf16[1,4,512,384]{3,1,0,2:T(4,128)(2,1)}, u32[]{:S(2)}, u32[]{:S(2)}) %all-to-all-start.1) | async-done | bytes 1572896 | tf_op jit(solution)/shard_map/all_to_all | solution.py:40
  83.7 9.8 %all-to-all-start = ((bf16[1,512,4,384]{3,2,0,1:T(4,128)(2,1)}), bf16[1,512,4,384]{3,2,0,1:T(4,128)(2,1)}, u32[]{:S(2)}, u32[]{:S(2)}) async-start(bf16[1,512,4,384]{3,2,0,1:T(4,128)(2,1)} %copy.25), calls=%async_computation | async-start | bytes 3145728 | tf_op jit(solution)/shard_map/all_to_all | solution.py:48
  93.6 3.1 %copy.32 = bf16[1,128,4,4,384]{4,2,1,3,0:T(4,128)(2,1)} copy(bf16[1,128,4,4,384]{4,2,3,1,0:T(4,128)(2,1)} %bitcast.14) | data formatting | bytes 3145728 | tf_op jit(solution)/shard_map/all_to_all | solution.py:40
  96.6 3.7 %reshape.110 = bf16[512,4,384]{2,0,1:T(8,128)(2,1)} reshape(bf16[1,128,4,4,384]{4,2,1,3,0:T(4,128)(2,1)} %copy.32) | data formatting | bytes 3145728 | tf_op jit(solution)/shard_map/reshape.23
  100.4 4.5 %convert_bitcast_fusion = bf16[4,512,512]{1,2,0:T(8,128)(2,1)} fusion(bf16[512,4,384]{2,0,1:T(8,128)(2,1)} %reshape.110, bf16[4,512,384]{2,1,0:T(8,128)(2,1)} %bitcast.41), kind=kOutput, calls=%fused_computation.21 | convolution fusion | flops 806354944 | bytes 5242880 | tf_op jit(solution)/shard_map/skmd,sikd->kmi/dot_general | solution.py:45
  105.1 31.8 %all-to-all-done = bf16[1,512,4,384]{3,2,0,1:T(4,128)(2,1)} async-done(((bf16[1,512,4,384]{3,2,0,1:T(4,128)(2,1)}), bf16[1,512,4,384]{3,2,0,1:T(4,128)(2,1)}, u32[]{:S(2)}, u32[]{:S(2)}) %all-to-all-start) | async-done | bytes 1572896 | tf_op jit(solution)/shard_map/all_to_all | solution.py:48
  136.8 2.1 copy.26
  140.1 2.6 convolution_convert_fusion
  142.8 4.2 %convolution_bitcast_fusion = f32[1,4,512,384]{2,3,1,0:T(8,128)} fusion(bf16[4,512,512]{2,1,0:T(8,128)(2,1)S(1)} %copy-done, bf16[4,512,384]{2,0,1:T(4,128)(2,1)} %bitcast.43), kind=kOutput, calls=%fused_computation.24 | convolution fusion | flops 805306368 | bytes 6815744 | tf_op jit(solution)/shard_map/ikj,sikd->sijd/dot_general | solution.py:49
  147.0 3.6 %copy.28 = f32[1,4,512,384]{3,2,1,0:T(8,128)} copy(f32[1,4,512,384]{2,3,1,0:T(8,128)} %convolution_bitcast_fusion) | data formatting | bytes 6291456 | tf_op jit(solution)/shard_map/ikj,sikd->sijd/transpose | solution.py:49
  150.6 4.0 %fusion.8 = bf16[1,2048,384]{2,1,0:T(8,128)(2,1)S(1)} fusion(f32[1,4,512,384]{3,2,1,0:T(8,128)} %copy.28, f32[1,2048,384]{2,1,0:T(8,128)} %get-tuple-element.17), kind=kLoop, calls=%fused_computation.17 | loop fusion | flops 7077888 | bytes 7864320 | tf_op jit(solution)/shard_map/convert_element_type | solution.py:52
  155.8 4.1 %collective-permute-start.1 = (bf16[1,3,384]{2,1,0:T(4,128)(2,1)S(1)}, bf16[1,3,384]{2,1,0:T(4,128)(2,1)S(1)}, u32[]{:S(2)}, u32[]{:S(2)}) collective-permute-start(bf16[1,3,384]{2,1,0:T(4,128)(2,1)S(1)} %slice.64), channel_id=1, source_target_pairs={{1,0},{2,1},{3,2},{4,3},{5,4},{6,5},{7,6},{8,7},{9,8},{10,9},{11,1... | collective-permute-start | bytes 6920 | tf_op jit(solution)/shard_map/ppermute | solution.py:15
  162.3 2.5 fusion.1
  164.8 25.2 %all-reduce.2.cloned.1.call-done = bf16[4,512,512]{1,2,0:T(8,128)(2,1)} async-done(((bf16[4,512,512]{1,2,0:T(8,128)(2,1)}), bf16[4,512,512]{1,2,0:T(8,128)(2,1)}) %all-reduce.2.cloned.1.call-update) | async-done | bytes 2097168 | tf_op jit(solution)/shard_map/psum | solution.py:63
  192.7 61.6 %all-gather.3.cloned.1.call-done = bf16[8,512,512]{2,1,0:T(8,128)(2,1)} async-done(((bf16[4,512,512]{2,1,0:T(8,128)(2,1)}), bf16[8,512,512]{2,1,0:T(8,128)(2,1)}) %all-gather.3.cloned.1.call-update) | async-done | bytes 4194320 | tf_op jit(solution)/shard_map/all_gather | solution.py:8
  254.3 4.9 %reduce_sum.12 = bf16[4,512,512]{2,1,0:T(8,128)(2,1)} reduce(bf16[2,4,512,512]{3,2,1,0:T(8,128)(2,1)} %bitcast.46, bf16[]{:T(256)} %constant.4.clone.1), dimensions={0}, to_apply=%region_0.0 | reduce | flops 1048576 | bytes 6291458 | tf_op jit(solution)/shard_map/reduce_sum | solution.py:8
  259.3 2.3 convert_convert_fusion.1
  (23 shorter events, 12.2 us)
Async XLA Ops:
  7.2 12.3 %copy-start = (bf16[4,512,512]{2,1,0:T(8,128)(2,1)S(1)}, bf16[4,512,512]{2,1,0:T(8,128)(2,1)}, u32[]{:S(2)}) copy-start(bf16[4,512,512]{2,1,0:T(8,128)(2,1)} %param.7) | copy-start | bytes 6291460
  8.0 5.4 %collective-permute-start = (bf16[1,3,384]{2,1,0:T(4,128)(2,1)S(1)}, bf16[1,3,384]{2,1,0:T(4,128)(2,1)S(1)}, u32[]{:S(2)}, u32[]{:S(2)}) collective-permute-start(bf16[1,3,384]{2,1,0:T(4,128)(2,1)S(1)} %slice.47), channel_id=1, source_target_pairs={{0,1},{1,2},{2,3},{3,4},{4,5},{5,6},{6,7},{7,8},{8,9},{9,10},{10,1... | collective-permute-start | bytes 6920 | tf_op jit(solution)/shard_map/ppermute | solution.py:15
  18.3 1.2 copy-start.3
  25.5 58.2 %all-to-all-start.1 = ((bf16[1,4,512,384]{3,1,0,2:T(4,128)(2,1)}), bf16[1,4,512,384]{3,1,0,2:T(4,128)(2,1)}, u32[]{:S(2)}, u32[]{:S(2)}) async-start(bf16[1,4,512,384]{3,1,0,2:T(4,128)(2,1)} %copy.31), calls=%async_computation.1 | async-start | bytes 3145728 | tf_op jit(solution)/shard_map/all_to_all | solution.py:40
  83.7 53.1 %all-to-all-start = ((bf16[1,512,4,384]{3,2,0,1:T(4,128)(2,1)}), bf16[1,512,4,384]{3,2,0,1:T(4,128)(2,1)}, u32[]{:S(2)}, u32[]{:S(2)}) async-start(bf16[1,512,4,384]{3,2,0,1:T(4,128)(2,1)} %copy.25), calls=%async_computation | async-start | bytes 3145728 | tf_op jit(solution)/shard_map/all_to_all | solution.py:48
  93.5 96.6 %all-reduce.2.cloned.1.call-start = ((), (), s32[]{:S(2)}) async-start(), calls=%async_computation.2 | async-start | bytes 4194304 | tf_op jit(solution)/shard_map/psum | solution.py:63
  104.8 149.5 %all-gather.3.cloned.1.call-start = ((), (), s32[]{:S(2)}) async-start(), calls=%async_computation.3 | async-start | bytes 6291456 | tf_op jit(solution)/shard_map/all_gather | solution.py:8
  136.8 3.3 %copy-start.4 = (bf16[1,2048,384]{2,1,0:T(8,128)(2,1)S(1)}, bf16[1,2048,384]{2,1,0:T(8,128)(2,1)}, u32[]{:S(2)}) copy-start(bf16[1,2048,384]{2,1,0:T(8,128)(2,1)} %copy-done.3) | copy-start | bytes 4718596
  139.0 1.1 copy-start.2
  154.6 1.1 copy-start.1
  155.8 4.9 %collective-permute-start.1 = (bf16[1,3,384]{2,1,0:T(4,128)(2,1)S(1)}, bf16[1,3,384]{2,1,0:T(4,128)(2,1)S(1)}, u32[]{:S(2)}, u32[]{:S(2)}) collective-permute-start(bf16[1,3,384]{2,1,0:T(4,128)(2,1)S(1)} %slice.64), channel_id=1, source_target_pairs={{1,0},{2,1},{3,2},{4,3},{5,4},{6,5},{7,6},{8,7},{9,8},{10,9},{11,1... | collective-permute-start | bytes 6920 | tf_op jit(solution)/shard_map/ppermute | solution.py:15
Sparse Core Ops, SparseCore 0:
  105.0 85.0 all-reduce.1
  192.0 62.2 all-gather.2
